TPU v7x, 128 devices: a whole 4x4x4 slice. The times are simulated.
128 devices in a mesh: dp: 64 (over z, y, x), tensor: 2 (over core).
Axes of the slice: x: 4, y: 4, z: 4, core: 2. Of those that a mesh axis runs over, the one named last changes fastest.
Arguments:
- tokens: bfloat16 [49152, 768], P(('dp', 'tensor')), may hold values from -6 to 6
- skip_tokens: bfloat16 [49152, 768], P(('dp', 'tensor')), may hold values from -6 to 6
- cot_back: bfloat16 [49152, 768], P(('dp', 'tensor')), may hold values from -6 to 6
- cot_head: bfloat16 [49152, 768], P(('dp', 'tensor')), may hold values from -6 to 6
- one_span: int32 [192], P('dp'), may hold values 0 or 1
- lower_qkv: bfloat16 [3, 768, 768], P(None, None, 'tensor'), may hold values from -0.21875 to 0.21875
- lower_proj: bfloat16 [768, 768], P('tensor'), may hold values from -1.75 to 1.75
- lower_gain_attn: float32 [768], replicated, may hold values from 0.1 to 1.9
- lower_shift_attn: float32 [768], replicated, may hold values from -1.5 to 1.5
- lower_w_in: bfloat16 [768, 3072], P(None, 'tensor'), may hold values from -0.21875 to 0.21875
- lower_w_out: bfloat16 [3072, 768], P('tensor'), may hold values from -0.15625 to 0.15625
- lower_gain_ffn: float32 [768], replicated, may hold values from 0.1 to 1.9
- lower_shift_ffn: float32 [768], replicated, may hold values from -1.5 to 1.5
- upper_qkv: bfloat16 [3, 768, 768], P(None, None, 'tensor'), may hold values from -0.21875 to 0.21875
- upper_proj: bfloat16 [768, 768], P('tensor'), may hold values from -1.75 to 1.75
- upper_gain_attn: float32 [768], replicated, may hold values from 0.1 to 1.9
- upper_shift_attn: float32 [768], replicated, may hold values from -1.5 to 1.5
- upper_w_in: bfloat16 [768, 3072], P(None, 'tensor'), may hold values from -0.21875 to 0.21875
- upper_w_out: bfloat16 [3072, 768], P('tensor'), may hold values from -0.15625 to 0.15625
- upper_gain_ffn: float32 [768], replicated, may hold values from 0.1 to 1.9
- upper_shift_ffn: float32 [768], replicated, may hold values from -1.5 to 1.5
Outputs:
- back_out: bfloat16 [49152, 768], P(('dp', 'tensor'))
- head_out: bfloat16 [49152, 768], P(('dp', 'tensor'))
- grad_tokens: float32 [49152, 768], P(('dp', 'tensor'))
- grad_skip: float32 [49152, 768], P(('dp', 'tensor'))
- grad_lower_qkv: float32 [3, 768, 768], P(None, None, 'tensor')
- grad_lower_proj: float32 [768, 768], P('tensor')
- grad_lower_gain_attn: float32 [768], replicated
- grad_lower_shift_attn: float32 [768], replicated
- grad_lower_w_in: float32 [768, 3072], P(None, 'tensor')
- grad_lower_w_out: float32 [3072, 768], P('tensor')
- grad_lower_gain_ffn: float32 [768], replicated
- grad_lower_shift_ffn: float32 [768], replicated
- grad_upper_qkv: float32 [3, 768, 768], P(None, None, 'tensor')
- grad_upper_proj: float32 [768, 768], P('tensor')
- grad_upper_gain_attn: float32 [768], replicated
- grad_upper_shift_attn: float32 [768], replicated
- grad_upper_w_in: float32 [768, 3072], P(None, 'tensor')
- grad_upper_w_out: float32 [3072, 768], P('tensor')
- grad_upper_gain_ffn: float32 [768], replicated
- grad_upper_shift_ffn: float32 [768], replicated
Inputs may be any that keep to these rules, and one draw needn't show every extreme that they name: `one_span`: 1 marks a document whose second span is padding: masked as keys, and zero in both outputs.
All inputs are finite; a program needn't handle non-finite values. No bound on the sum of `one_span` on one device may be relied on, other than what follows from the above.
Results may differ from a plain program's by a relative error of at most 0.02.
Values may be sent and summed in bfloat16 or wider, within the bound.
No kernel may reach another device: no remote copies, remote signals or barrier semaphores. Data moves between devices by JAX's collectives and lax.ppermute only.
A program may use at most 192 MiB of HBM per device.

v0:
```python
import jax
import jax.numpy as jnp
from jax import lax
from jax.sharding import PartitionSpec as P

HEAD_DIM = 64
SPAN = 128
EPS = 1e-06
SCALE = 0.125
NEG = -1000000000.0


def norm_forward(resid, gain, shift):
    mean = jnp.mean(resid, axis=-1, keepdims=True)
    centered = resid - mean
    var = jnp.mean(centered * centered, axis=-1, keepdims=True)
    inv_std = lax.rsqrt(var + EPS)
    normed = centered * inv_std
    return (normed * gain + shift, normed, inv_std)


def norm_backward(grad_out, normed, inv_std, gain):
    grad_normed = grad_out * gain
    first_mean = jnp.mean(grad_normed, axis=-1, keepdims=True)
    second_mean = jnp.mean(grad_normed * normed, axis=-1, keepdims=True)
    grad_resid = inv_std * (grad_normed - first_mean - normed * second_mean)
    return (grad_resid, jnp.sum(grad_out * normed, axis=0), jnp.sum(grad_out, axis=0))


def gelu_slope(value):
    return (
        0.5 * (1.0 + jax.scipy.special.erf(value * 0.7071067811865476))
        + value * jnp.exp(-0.5 * value * value) * 0.3989422804014327
    )


def contract_last(left, right):
    return lax.dot_general(
        left, right, (((1,), (1,)), ((), ())), preferred_element_type=jnp.float32
    )


def contract_rows(left, right):
    return lax.dot_general(
        left, right, (((0,), (0,)), ((), ())), preferred_element_type=jnp.float32
    )


def gather_rows(rows_low):
    return lax.all_gather(rows_low, "tensor", axis=0, tiled=True)


def gather_grad(rows_low):
    return lax.all_gather(rows_low, "tensor", axis=0, tiled=True)


def sum_rows(full, weight, count):

    def term(start, size):
        return jnp.dot(full, weight, preferred_element_type=jnp.float32)

    return lax.psum_scatter(
        term(jnp.int32(0), count * lax.axis_size("tensor")).astype(jnp.bfloat16),
        "tensor",
        scatter_dimension=0,
        tiled=True,
    ).astype(jnp.float32)


def sum_back(term, count):
    return lax.psum_scatter(
        term(jnp.int32(0), count * lax.axis_size("tensor")).astype(jnp.bfloat16),
        "tensor",
        scatter_dimension=0,
        tiled=True,
    ).astype(jnp.float32)


def split_heads(full_qkv, index, docs):
    rows, _, width = full_qkv.shape
    return full_qkv[:, index].reshape(docs, 2 * SPAN, width // HEAD_DIM, HEAD_DIM)


def attend(qkv, key_ok):
    docs = key_ok.shape[0]
    rows, _, width = qkv.shape
    query = split_heads(qkv, 0, docs).astype(jnp.bfloat16)
    keys = split_heads(qkv, 1, docs).astype(jnp.bfloat16)
    values = split_heads(qkv, 2, docs).astype(jnp.bfloat16)
    scores = jnp.einsum("nqhe,nkhe->nhqk", query, keys, preferred_element_type=jnp.float32) * SCALE
    scores = jnp.where(key_ok[:, None, None, :], scores, NEG)
    largest = jnp.max(scores, axis=-1, keepdims=True)
    raised = jnp.exp(scores - largest)
    total = jnp.sum(raised, axis=-1, keepdims=True)
    log_total = largest + jnp.log(total)
    prob_low = (raised / total).astype(jnp.bfloat16)
    mixed = jnp.einsum("nhqk,nkhe->nqhe", prob_low, values, preferred_element_type=jnp.float32)
    context = mixed.reshape(rows, width).astype(jnp.bfloat16)
    return (context, (query, keys, values, log_total))


def attend_back(grad_ctx, kept, key_ok):
    query, keys, values, log_total = kept
    docs, length, heads, size = query.shape
    scores = jnp.einsum("nqhe,nkhe->nhqk", query, keys, preferred_element_type=jnp.float32) * SCALE
    scores = jnp.where(key_ok[:, None, None, :], scores, NEG)
    prob = jnp.exp(scores - log_total)
    prob_low = prob.astype(jnp.bfloat16)
    grad_mix = grad_ctx.reshape(docs, length, heads, size)
    grad_values = jnp.einsum(
        "nhqk,nqhe->nkhe", prob_low, grad_mix, preferred_element_type=jnp.float32
    )
    grad_prob = jnp.einsum("nqhe,nkhe->nhqk", grad_mix, values, preferred_element_type=jnp.float32)
    grad_scores = prob * (grad_prob - jnp.sum(grad_prob * prob, axis=-1, keepdims=True))
    grad_scores = grad_scores.astype(jnp.bfloat16)
    grad_query = (
        jnp.einsum("nhqk,nkhe->nqhe", grad_scores, keys, preferred_element_type=jnp.float32) * SCALE
    )
    grad_keys = (
        jnp.einsum("nhqk,nqhe->nkhe", grad_scores, query, preferred_element_type=jnp.float32)
        * SCALE
    )
    rows = docs * length
    width = heads * size
    stacked = jnp.stack(
        [
            grad_query.reshape(rows, width),
            grad_keys.reshape(rows, width),
            grad_values.reshape(rows, width),
        ],
        axis=1,
    )
    return stacked.astype(jnp.bfloat16)


def block_forward(rows, weights, key_ok, count):
    qkv_w, proj_w, gain_a, shift_a, in_w, out_w, gain_f, shift_f = weights
    full = gather_rows(rows.astype(jnp.bfloat16))
    qkv = jnp.einsum("rd,cdj->rcj", full, qkv_w, preferred_element_type=jnp.float32)
    context, att_kept = attend(qkv, key_ok)
    attn = sum_rows(context, proj_w, count)
    first, normed_a, inv_a = norm_forward(rows + attn, gain_a, shift_a)
    full_first = gather_rows(first.astype(jnp.bfloat16))
    pre = jnp.dot(full_first, in_w, preferred_element_type=jnp.float32)
    act = jax.nn.gelu(pre, approximate=False).astype(jnp.bfloat16)
    ffn = sum_rows(act, out_w, count)
    result, normed_f, inv_f = norm_forward(first + ffn, gain_f, shift_f)
    return (
        result,
        (full, att_kept, context, normed_a, inv_a, full_first, pre, act, normed_f, inv_f),
    )


def block_backward(grad_out, weights, key_ok, count, kept):
    qkv_w, proj_w, gain_a, shift_a, in_w, out_w, gain_f, shift_f = weights
    full, att_kept, context, normed_a, inv_a, full_first, pre, act, normed_f, inv_f = kept
    grad_second, grad_gain_f, grad_shift_f = norm_backward(grad_out, normed_f, inv_f, gain_f)
    full_grad_ffn = gather_grad(grad_second.astype(jnp.bfloat16))
    grad_act = contract_last(full_grad_ffn, out_w)
    grad_out_w = contract_rows(act, full_grad_ffn)
    grad_pre = (grad_act * gelu_slope(pre)).astype(jnp.bfloat16)
    grad_in_w = contract_rows(full_first, grad_pre)

    def ffn_term(start, size):
        return contract_last(grad_pre, in_w)

    grad_first = grad_second + sum_back(ffn_term, count)
    grad_resid, grad_gain_a, grad_shift_a = norm_backward(grad_first, normed_a, inv_a, gain_a)
    full_grad_attn = gather_grad(grad_resid.astype(jnp.bfloat16))
    grad_ctx = contract_last(full_grad_attn, proj_w).astype(jnp.bfloat16)
    grad_proj = contract_rows(context, full_grad_attn)
    grad_qkv = attend_back(grad_ctx, att_kept, key_ok)
    grad_qkv_w = jnp.einsum("rd,rcj->cdj", full, grad_qkv, preferred_element_type=jnp.float32)

    def attn_term(start, size):
        return jnp.einsum("rcj,cdj->rd", grad_qkv, qkv_w, preferred_element_type=jnp.float32)

    grad_rows = grad_resid + sum_back(attn_term, count)
    return (
        grad_rows,
        (grad_qkv_w, grad_proj, grad_in_w, grad_out_w),
        (grad_gain_a, grad_shift_a, grad_gain_f, grad_shift_f),
    )


def on_device(
    tokens,
    skip_tokens,
    cot_back,
    cot_head,
    one_span,
    lower_qkv,
    lower_proj,
    lower_gain_attn,
    lower_shift_attn,
    lower_w_in,
    lower_w_out,
    lower_gain_ffn,
    lower_shift_ffn,
    upper_qkv,
    upper_proj,
    upper_gain_attn,
    upper_shift_attn,
    upper_w_in,
    upper_w_out,
    upper_gain_ffn,
    upper_shift_ffn,
):
    count = tokens.shape[0]
    docs_local = one_span.shape[0]
    position = jnp.arange(2 * SPAN)
    key_ok = (position[None, :] < SPAN) | (one_span[:, None] == 0)
    row_index = lax.axis_index("tensor") * count + jnp.arange(count)
    doc_index = row_index // (2 * SPAN)
    doc_flag = jnp.sum(
        jnp.where(doc_index[:, None] == jnp.arange(docs_local)[None, :], one_span[None, :], 0),
        axis=1,
    )
    row_ok = (row_index // SPAN % 2 == 0) | (doc_flag == 0)
    valid = row_ok[:, None].astype(jnp.float32)
    is_cls = (row_index % SPAN == 0)[:, None]
    lower = (
        lower_qkv,
        lower_proj,
        lower_gain_attn,
        lower_shift_attn,
        lower_w_in,
        lower_w_out,
        lower_gain_ffn,
        lower_shift_ffn,
    )
    upper = (
        upper_qkv,
        upper_proj,
        upper_gain_attn,
        upper_shift_attn,
        upper_w_in,
        upper_w_out,
        upper_gain_ffn,
        upper_shift_ffn,
    )
    back, kept_lower = block_forward(tokens.astype(jnp.float32), lower, key_ok, count)
    head_in = jnp.where(is_cls, back, skip_tokens.astype(jnp.float32))
    head, kept_upper = block_forward(head_in, upper, key_ok, count)
    head_again, kept_upper = block_forward(head_in, upper, key_ok, count)
    grad_head_in, weights_upper, norms_upper = block_backward(
        cot_head.astype(jnp.float32) * valid, upper, key_ok, count, kept_upper
    )
    grad_skip = jnp.where(is_cls, 0.0, grad_head_in)
    grad_back = cot_back.astype(jnp.float32) * valid + jnp.where(is_cls, grad_head_in, 0.0)
    back_again, kept_lower = block_forward(tokens.astype(jnp.float32), lower, key_ok, count)
    grad_tokens, weights_lower, norms_lower = block_backward(
        grad_back, lower, key_ok, count, kept_lower
    )
    summed = lax.psum(
        (
            weights_lower[0],
            weights_lower[1],
            weights_lower[2],
            weights_lower[3],
            weights_upper[0],
            weights_upper[1],
            weights_upper[2],
            weights_upper[3],
        ),
        "dp",
    )
    weights_lower = summed[:4]
    weights_upper = summed[4:]
    norms = lax.psum(
        (
            norms_lower[0],
            norms_lower[1],
            norms_lower[2],
            norms_lower[3],
            norms_upper[0],
            norms_upper[1],
            norms_upper[2],
            norms_upper[3],
        ),
        ("dp", "tensor"),
    )
    return (
        (back * valid).astype(jnp.bfloat16),
        (head * valid).astype(jnp.bfloat16),
        grad_tokens,
        grad_skip,
        weights_lower[0],
        weights_lower[1],
        norms[0],
        norms[1],
        weights_lower[2],
        weights_lower[3],
        norms[2],
        norms[3],
        weights_upper[0],
        weights_upper[1],
        norms[4],
        norms[5],
        weights_upper[2],
        weights_upper[3],
        norms[6],
        norms[7],
    )


def solution(mesh):
    return jax.shard_map(
        on_device,
        mesh=mesh,
        in_specs=(
            P(("dp", "tensor"), None),
            P(("dp", "tensor"), None),
            P(("dp", "tensor"), None),
            P(("dp", "tensor"), None),
            P("dp"),
            P(None, None, "tensor"),
            P("tensor", None),
            P(),
            P(),
            P(None, "tensor"),
            P("tensor", None),
            P(),
            P(),
            P(None, None, "tensor"),
            P("tensor", None),
            P(),
            P(),
            P(None, "tensor"),
            P("tensor", None),
            P(),
            P(),
        ),
        out_specs=(
            P(("dp", "tensor"), None),
            P(("dp", "tensor"), None),
            P(("dp", "tensor"), None),
            P(("dp", "tensor"), None),
            P(None, None, "tensor"),
            P("tensor", None),
            P(),
            P(),
            P(None, "tensor"),
            P("tensor", None),
            P(),
            P(),
            P(None, None, "tensor"),
            P("tensor", None),
            P(),
            P(),
            P(None, "tensor"),
            P("tensor", None),
            P(),
            P(),
        ),
        check_vma=False,
    )
```

profile of v0, /device:TPU:1, one launch (start us, length us, event | category | flops | bytes accessed | tf_op | source)
XLA Modules:
  0.0 769.2 jit_solution(13849110559285241744)
XLA Ops:
  8.7 16.6 %all-gather.9.cloned.1.call-done = bf16[768,768]{1,0:T(8,128)(2,1)} async-done(((bf16[384,768]{1,0:T(8,128)(2,1)}), bf16[768,768]{1,0:T(8,128)(2,1)}) %all-gather.9.cloned.1.call-update) | async-done | bytes 1179664 | tf_op jit(solution)/shard_map/all_gather | solution.py:50
  25.3 3.5 convolution_convert_fusion.1
  50.5 12.8 %reduce-scatter.9.cloned.1.call-done = bf16[384,768]{1,0:T(8,128)(2,1)} async-done(((bf16[768,768]{1,0:T(8,128)(2,1)}), bf16[384,768]{1,0:T(8,128)(2,1)}) %reduce-scatter.9.cloned.1.call-update) | async-done | bytes 589840 | tf_op jit(solution)/shard_map/reduce_scatter | solution.py:62
  67.8 12.9 %all-gather.11.cloned.1.call-done = bf16[768,768]{1,0:T(8,128)(2,1)} async-done(((bf16[384,768]{1,0:T(8,128)(2,1)}), bf16[768,768]{1,0:T(8,128)(2,1)}) %all-gather.11.cloned.1.call-update) | async-done | bytes 1179664 | tf_op jit(solution)/shard_map/all_gather | solution.py:50
  80.7 14.4 %fusion.2 = (bf16[768,1536]{1,0:T(8,128)(2,1)S(1)}, f32[768,1536]{1,0:T(8,128)}) fusion(bf16[768,768]{1,0:T(8,128)(2,1)} %all-gather.11.cloned.1.call-done, bf16[768,1536]{1,0:T(8,128)(2,1)} %param.30), kind=kOutput, calls=%fused_computation.6 | convolution fusion | flops 1888616448 | bytes 10616832 | tf_op jit(solution)/shard_map/dot_general | solution.py:144
  100.1 12.3 %reduce-scatter.11.cloned.1.call-done = bf16[384,768]{1,0:T(8,128)(2,1)} async-done(((bf16[768,768]{1,0:T(8,128)(2,1)}), bf16[384,768]{1,0:T(8,128)(2,1)}) %reduce-scatter.11.cloned.1.call-update) | async-done | bytes 589840 | tf_op jit(solution)/shard_map/reduce_scatter | solution.py:62
  118.6 13.2 %all-gather.13.cloned.1.call-done = bf16[768,768]{1,0:T(8,128)(2,1)} async-done(((bf16[384,768]{1,0:T(8,128)(2,1)}), bf16[768,768]{1,0:T(8,128)(2,1)}) %all-gather.13.cloned.1.call-update) | async-done | bytes 1179664 | tf_op jit(solution)/shard_map/all_gather | solution.py:50
  163.4 11.5 %reduce-scatter.13.cloned.1.call-done = bf16[384,768]{1,0:T(8,128)(2,1)} async-done(((bf16[768,768]{1,0:T(8,128)(2,1)}), bf16[384,768]{1,0:T(8,128)(2,1)}) %reduce-scatter.13.cloned.1.call-update) | async-done | bytes 589840 | tf_op jit(solution)/shard_map/reduce_scatter | solution.py:62
  180.7 13.2 %all-gather.15.cloned.1.call-done = bf16[768,768]{1,0:T(8,128)(2,1)} async-done(((bf16[384,768]{1,0:T(8,128)(2,1)}), bf16[768,768]{1,0:T(8,128)(2,1)}) %all-gather.15.cloned.1.call-update) | async-done | bytes 1179664 | tf_op jit(solution)/shard_map/all_gather | solution.py:50
  193.9 13.7 %fusion.5 = (bf16[768,1536]{1,0:T(8,128)(2,1)S(1)}, f32[768,1536]{1,0:T(8,128)}) fusion(bf16[768,768]{1,0:T(8,128)(2,1)} %all-gather.15.cloned.1.call-done, bf16[768,1536]{1,0:T(8,128)(2,1)S(1)} %copy-done), kind=kOutput, calls=%fused_computation.9 | convolution fusion | flops 1888616448 | bytes 10616832 | tf_op jit(solution)/shard_map/dot_general | solution.py:144
  212.1 12.8 %reduce-scatter.15.cloned.1.call-done = bf16[384,768]{1,0:T(8,128)(2,1)} async-done(((bf16[768,768]{1,0:T(8,128)(2,1)}), bf16[384,768]{1,0:T(8,128)(2,1)}) %reduce-scatter.15.cloned.1.call-update) | async-done | bytes 589840 | tf_op jit(solution)/shard_map/reduce_scatter | solution.py:62
  232.0 13.4 %all-gather.17.cloned.1.call-done = bf16[768,768]{1,0:T(8,128)(2,1)} async-done(((bf16[384,768]{1,0:T(8,128)(2,1)}), bf16[768,768]{1,0:T(8,128)(2,1)}) %all-gather.17.cloned.1.call-update) | async-done | bytes 1179664 | tf_op jit(solution)/shard_map/all_gather | solution.py:54
  245.3 5.4 fusion.11
  255.2 12.8 %reduce-scatter.17.cloned.1.call-done = bf16[384,768]{1,0:T(8,128)(2,1)} async-done(((bf16[768,768]{1,0:T(8,128)(2,1)}), bf16[384,768]{1,0:T(8,128)(2,1)}) %reduce-scatter.17.cloned.1.call-update) | async-done | bytes 589840 | tf_op jit(solution)/shard_map/reduce_scatter | solution.py:71
  274.8 12.2 %all-gather.19.cloned.1.call-done = bf16[768,768]{1,0:T(8,128)(2,1)} async-done(((bf16[384,768]{1,0:T(8,128)(2,1)}), bf16[768,768]{1,0:T(8,128)(2,1)}) %all-gather.19.cloned.1.call-update) | async-done | bytes 1179664 | tf_op jit(solution)/shard_map/all_gather | solution.py:54
  290.9 4.2 fusion.65
  319.0 12.8 %reduce-scatter.19.cloned.1.call-done = bf16[384,768]{1,0:T(8,128)(2,1)} async-done(((bf16[768,768]{1,0:T(8,128)(2,1)}), bf16[384,768]{1,0:T(8,128)(2,1)}) %reduce-scatter.19.cloned.1.call-update) | async-done | bytes 589840 | tf_op jit(solution)/shard_map/reduce_scatter | solution.py:71
  331.9 3.5 multiply_reduce_fusion.4
  336.8 13.2 %all-gather.21.cloned.1.call-done = bf16[768,768]{1,0:T(8,128)(2,1)} async-done(((bf16[384,768]{1,0:T(8,128)(2,1)}), bf16[768,768]{1,0:T(8,128)(2,1)}) %all-gather.21.cloned.1.call-update) | async-done | bytes 1179664 | tf_op jit(solution)/shard_map/all_gather | solution.py:54
  350.0 5.5 fusion.17
  360.0 12.8 %reduce-scatter.21.cloned.1.call-done = bf16[384,768]{1,0:T(8,128)(2,1)} async-done(((bf16[768,768]{1,0:T(8,128)(2,1)}), bf16[384,768]{1,0:T(8,128)(2,1)}) %reduce-scatter.21.cloned.1.call-update) | async-done | bytes 589840 | tf_op jit(solution)/shard_map/reduce_scatter | solution.py:71
  377.1 6.4 fusion.109
  383.5 4.2 fusion.108
  394.5 4.2 fusion.62
  419.3 5.0 convolution_bitcast_fusion
  424.3 4.3 fusion.106
  428.6 4.2 fusion.105
  439.2 69.9 %all-reduce = (f32[768]{0:T(1024)}, f32[768]{0:T(1024)}, f32[768]{0:T(1024)}, f32[768]{0:T(1024)}, f32[768]{0:T(1024)}, /*index=5*/f32[768]{0:T(1024)}, f32[768]{0:T(1024)}, f32[768]{0:T(1024)}) all-reduce(f32[768]{0:T(1024)S(1)} %get-tuple-element.82, f32[768]{0:T(1024)S(1)} %copy-done.68, ...), channel_id=1, replica_groups=mesh['dp'=64,'tensor'=2] {'dp','tensor'}, use_global_device_ids=true, to_apply=%region_34.35 | all-reduce | flops 6144 | bytes 49152 | tf_op jit(solution)/shard_map/psum | solution.py:270
  511.3 223.8 %all-reduce.4.cloned.1.call-done = (f32[3,768,384]{1,2,0:T(8,128)}, f32[384,768]{1,0:T(8,128)}, f32[768,1536]{1,0:T(8,128)}, f32[1536,768]{1,0:T(8,128)}, f32[3,...) async-done(((f32[3,768,384]{1,2,0:T(8,128)}, f32[384,768]{1,0:T(8,128)}, f32[768,1536]{1,0:T(8,128)}, f32[1536,768]{1,0:T(8,128)}, ...) | async-done | bytes 28311568 | tf_op jit(solution)/shard_map/psum | solution.py:255
  735.1 5.2 copy.167
  740.3 5.3 copy.168
  746.6 5.5 copy.222
  (353 shorter events, 183.3 us)
Async XLA Ops:
  7.2 186.7 %copy-start = (bf16[768,1536]{1,0:T(8,128)(2,1)S(1)}, bf16[768,1536]{1,0:T(8,128)(2,1)}, u32[]{:S(2)}) copy-start(bf16[768,1536]{1,0:T(8,128)(2,1)} %param.38) | copy-start | bytes 7077892
  7.2 18.1 %all-gather.9.cloned.1.call-start = ((), (), s32[]{:S(2)}) async-start(), calls=%async_computation.8 | async-start | bytes 1769472 | tf_op jit(solution)/shard_map/all_gather | solution.py:50
  7.9 55.3 %reduce-scatter.9.cloned.1.call-start = ((), (), s32[]{:S(2)}) async-start(), calls=%async_computation.9 | async-start | bytes 1769472 | tf_op jit(solution)/shard_map/reduce_scatter | solution.py:62
  8.7 34.0 %copy-start.71 = (pred[3,256]{1,0:T(4,128)(4,1)}, pred[3,256]{1,0:T(4,128)(4,1)S(1)}, u32[]{:S(2)}) copy-start(pred[3,256]{1,0:T(4,128)(4,1)S(1)} %broadcast_or_fusion) | copy-start | bytes 2308
  47.6 15.6 %copy-start.4 = (bf16[384,768]{1,0:T(8,128)(2,1)S(1)}, bf16[384,768]{1,0:T(8,128)(2,1)}, u32[]{:S(2)}) copy-start(bf16[384,768]{1,0:T(8,128)(2,1)} %param.21) | copy-start | bytes 1769476
  50.4 15.7 %copy-start.52 = (f32[768]{0:T(1024)S(1)}, f32[768]{0:T(1024)}, u32[]{:S(2)}) copy-start(f32[768]{0:T(1024)} %param.28) | copy-start | bytes 9220
  50.4 15.7 %copy-start.56 = (f32[768]{0:T(1024)S(1)}, f32[768]{0:T(1024)}, u32[]{:S(2)}) copy-start(f32[768]{0:T(1024)} %param.29) | copy-start | bytes 9220
  50.4 30.2 %all-gather.11.cloned.1.call-start = ((), (), s32[]{:S(2)}) async-start(), calls=%async_computation.10 | async-start | bytes 1769472 | tf_op jit(solution)/shard_map/all_gather | solution.py:50
  67.2 45.1 %reduce-scatter.11.cloned.1.call-start = ((), (), s32[]{:S(2)}) async-start(), calls=%async_computation.11 | async-start | bytes 1769472 | tf_op jit(solution)/shard_map/reduce_scatter | solution.py:62
  80.7 15.8 %copy-start.75 = (bf16[1536,768]{1,0:T(8,128)(2,1)S(1)}, bf16[1536,768]{1,0:T(8,128)(2,1)}, u32[]{:S(2)}) copy-start(bf16[1536,768]{1,0:T(8,128)(2,1)} %param.31) | copy-start | bytes 7077892
  99.5 32.3 %all-gather.13.cloned.1.call-start = ((), (), s32[]{:S(2)}) async-start(), calls=%async_computation.12 | async-start | bytes 1769472 | tf_op jit(solution)/shard_map/all_gather | solution.py:50
  118.4 56.5 %reduce-scatter.13.cloned.1.call-start = ((), (), s32[]{:S(2)}) async-start(), calls=%async_computation.13 | async-start | bytes 1769472 | tf_op jit(solution)/shard_map/reduce_scatter | solution.py:62
  159.2 15.7 %copy-start.58 = (f32[768]{0:T(1024)S(1)}, f32[768]{0:T(1024)}, u32[]{:S(2)}) copy-start(f32[768]{0:T(1024)} %param.32) | copy-start | bytes 9220
  162.0 31.8 %all-gather.15.cloned.1.call-start = ((), (), s32[]{:S(2)}) async-start(), calls=%async_computation.14 | async-start | bytes 1769472 | tf_op jit(solution)/shard_map/all_gather | solution.py:50
  180.4 44.5 %reduce-scatter.15.cloned.1.call-start = ((), (), s32[]{:S(2)}) async-start(), calls=%async_computation.15 | async-start | bytes 1769472 | tf_op jit(solution)/shard_map/reduce_scatter | solution.py:62
  193.9 15.2 %copy-start.74 = (bf16[1536,768]{1,0:T(8,128)(2,1)S(1)}, bf16[1536,768]{1,0:T(8,128)(2,1)}, u32[]{:S(2)}) copy-start(bf16[1536,768]{1,0:T(8,128)(2,1)} %param.39) | copy-start | bytes 7077892
  212.0 33.3 %all-gather.17.cloned.1.call-start = ((), (), s32[]{:S(2)}) async-start(), calls=%async_computation.16 | async-start | bytes 1769472 | tf_op jit(solution)/shard_map/all_gather | solution.py:54
  231.9 36.1 %reduce-scatter.17.cloned.1.call-start = ((), (), s32[]{:S(2)}) async-start(), calls=%async_computation.17 | async-start | bytes 1769472 | tf_op jit(solution)/shard_map/reduce_scatter | solution.py:71
  255.2 16.0 %copy-start.6 = (f32[384,768]{1,0:T(8,128)S(1)}, f32[384,768]{1,0:T(8,128)}, u32[]{:S(2)}) copy-start(f32[384,768]{1,0:T(8,128)} %copy-done.5) | copy-start | bytes 3538948
  255.2 16.0 %copy-start.9 = (f32[384,768]{1,0:T(8,128)S(1)}, f32[384,768]{1,0:T(8,128)}, u32[]{:S(2)}) copy-start(f32[384,768]{1,0:T(8,128)} %get-tuple-element.120) | copy-start | bytes 3538948
  255.2 31.8 %all-gather.19.cloned.1.call-start = ((), (), s32[]{:S(2)}) async-start(), calls=%async_computation.18 | async-start | bytes 1769472 | tf_op jit(solution)/shard_map/all_gather | solution.py:54
  273.5 58.3 %reduce-scatter.19.cloned.1.call-start = ((), (), s32[]{:S(2)}) async-start(), calls=%async_computation.19 | async-start | bytes 1769472 | tf_op jit(solution)/shard_map/reduce_scatter | solution.py:71
  274.7 20.4 %copy-start.45 = (f32[3,6,256]{2,1,0:T(8,128)}, f32[3,6,256]{2,1,0:T(8,128)S(1)}, u32[]{:S(2)}) copy-start(f32[3,6,256]{2,1,0:T(8,128)S(1)} %log_add_fusion.1) | copy-start | bytes 55300
  316.2 15.6 %copy-start.8 = (f32[384,768]{1,0:T(8,128)S(1)}, f32[384,768]{1,0:T(8,128)}, u32[]{:S(2)}) copy-start(f32[384,768]{1,0:T(8,128)} %get-tuple-element.126) | copy-start | bytes 3538948
  316.2 15.6 %copy-start.18 = (f32[384,768]{1,0:T(8,128)S(1)}, f32[384,768]{1,0:T(8,128)}, u32[]{:S(2)}) copy-start(f32[384,768]{1,0:T(8,128)} %get-tuple-element.118) | copy-start | bytes 3538948
  316.2 15.6 %copy-start.59 = (f32[768]{0:T(1024)S(1)}, f32[768]{0:T(1024)}, u32[]{:S(2)}) copy-start(f32[768]{0:T(1024)} %param.32) | copy-start | bytes 9220
  319.0 31.0 %all-gather.21.cloned.1.call-start = ((), (), s32[]{:S(2)}) async-start(), calls=%async_computation.20 | async-start | bytes 1769472 | tf_op jit(solution)/shard_map/all_gather | solution.py:54
  336.6 36.3 %reduce-scatter.21.cloned.1.call-start = ((), (), s32[]{:S(2)}) async-start(), calls=%async_computation.21 | async-start | bytes 1769472 | tf_op jit(solution)/shard_map/reduce_scatter | solution.py:71
  360.0 30.5 %all-gather.23.cloned.1.call-start = ((), (), s32[]{:S(2)}) async-start(), calls=%async_computation.22 | async-start | bytes 1769472 | tf_op jit(solution)/shard_map/all_gather | solution.py:54
  377.0 132.1 %reduce-scatter.23.cloned.1.call-start = ((), (), s32[]{:S(2)}) async-start(), calls=%async_computation.23 | async-start | bytes 1769472 | tf_op jit(solution)/shard_map/reduce_scatter | solution.py:71
  417.3 317.9 %all-reduce.4.cloned.1.call-start = ((), (), s32[]{:S(2)}) async-start(), calls=%async_computation.24 | async-start | bytes 56623104 | tf_op jit(solution)/shard_map/psum | solution.py:255
  438.5 70.7 %copy-start.17 = (f32[384,768]{1,0:T(8,128)S(1)}, f32[384,768]{1,0:T(8,128)}, u32[]{:S(2)}) copy-start(f32[384,768]{1,0:T(8,128)} %get-tuple-element.113) | copy-start | bytes 3538948
  (83 other events, 264.6 us)
Sparse Core Ops, SparseCore 0:
  9.7 15.5 all-gather.8
  50.5 12.6 reduce-scatter.8
  67.3 13.2 all-gather.10
  99.6 12.6 reduce-scatter.10
  118.5 13.2 all-gather.12
  162.1 12.7 reduce-scatter.12
  180.5 13.2 all-gather.14
  212.2 12.6 reduce-scatter.14
  232.0 13.2 all-gather.16
  255.3 12.6 reduce-scatter.16
  273.6 13.2 all-gather.18
  319.1 12.6 reduce-scatter.18
  336.7 13.2 all-gather.20
  360.1 12.6 reduce-scatter.20
  377.2 13.2 all-gather.22
  417.4 12.6 reduce-scatter.22
  438.6 296.4 all-reduce.3
where the time goes:
time: 777 us; the launch traced here: 769 us
  waiting for transfers between devices  410 us (53%)
  matrix products  128 us (16%)
  local copies, waits for them, and re-layouts  98.2 us (13%)
  blocking collectives  69.9 us (9%)
  other arithmetic  45.2 us (6%)
  between operations  15.4 us (2%)
    psum x1, waiting for transfers between devices, on_device(): lax.psum((weights_lower[0], weights_lower[1], weights_lower[2], weights_l...  224 us
    psum x1, blocking collectives, on_device(): lax.psum((norms_lower[0], norms_lower[1], norms_lower[2], norms_lower[3],...  69.9 us
    all_gather x4, waiting for transfers between devices, gather_rows(): return lax.all_gather(rows_low, 'tensor', axis=0, tiled=True)  55.8 us
    reduce_scatter x4, waiting for transfers between devices, sum_rows(): lax.psum_scatter(term(jnp.int32(0), count * lax.axis_size('tensor')).asty...  49.3 us
    unnamed x210, local copies, waits for them, and re-layouts  46 us
    all_gather x4, waiting for transfers between devices, gather_grad(): return lax.all_gather(rows_low, 'tensor', axis=0, tiled=True)  41.5 us
    reduce_scatter x4, waiting for transfers between devices, sum_back(): lax.psum_scatter(term(jnp.int32(0), count * lax.axis_size('tensor')).asty...  38.4 us
    dot_general x2, matrix products, block_forward(): pre = jnp.dot(full_first, in_w, preferred_element_type=jnp.float32)  28.1 us
  transfers between devices with their start and end apart: 17, of which 16 were waited for; matrix products, arithmetic and copies ran while one was open for 5% of the time, Pallas kernels for 0%

commit v1 on v0

--- a/solution.py
+++ b/solution.py
@@ -1,3 +1,4 @@
+import functools
 import jax
 import jax.numpy as jnp
 from jax import lax
@@ -8,6 +9,17 @@
 EPS = 1e-06
 SCALE = 0.125
 NEG = -1000000000.0
+
+
+def apply_stacks_all(z, at_axis):
+    by_place = []
+    for _ in range(lax.axis_size("tensor")):
+        by_place.append(z)
+    mat_out = jnp.concatenate(lax.all_to_all(jnp.stack(by_place), "tensor", 0, 0), axis=at_axis)
+    return mat_out
+
+
+tell_goods_over_axis = functools.partial(apply_stacks_all, at_axis=0)
 
 
 def norm_forward(resid, gain, shift):
@@ -47,7 +59,7 @@
 
 
 def gather_rows(rows_low):
-    return lax.all_gather(rows_low, "tensor", axis=0, tiled=True)
+    return tell_goods_over_axis(rows_low)
 
 
 def gather_grad(rows_low):

time: 777 us -> 737 us (0.949)
  waiting for transfers between devices: 410 us -> 357 us
  blocking collectives: 69.9 us -> 84.5 us
    all_gather x4 -> x0, waiting for transfers between devices: 55.8 us -> none  [gather_rows(): return lax.all_gather(rows_low, 'tensor', axis=0, tiled=True)]
    all_to_all x0 -> x3, blocking collectives: none -> 14.5 us  [apply_stacks_all(): lax.all_to_all(jnp.stack(by_place), 'tensor', 0, 0)]
    unnamed x210 -> x228, local copies, waits for them, and re-layouts: 46 us -> 44.8 us
  transfers between devices with their start and end apart: 17 -> 14, of which waited for: 16 -> 13; matrix products, arithmetic and copies ran while one was open for 5% -> 5% of each run, Pallas kernels for 0% -> 0%
where the time goes in v1:
time: 737 us; the launch traced here: 729 us
  waiting for transfers between devices  357 us (48%)
  matrix products  125 us (17%)
  local copies, waits for them, and re-layouts  97.3 us (13%)
  blocking collectives  84.5 us (11%)
  other arithmetic  43.4 us (6%)
  between operations  15.2 us (2%)
    psum x1, waiting for transfers between devices, on_device(): lax.psum((weights_lower[0], weights_lower[1], weights_lower[2], weights_l...  224 us
    psum x1, blocking collectives, on_device(): lax.psum((norms_lower[0], norms_lower[1], norms_lower[2], norms_lower[3],...  70 us
    reduce_scatter x4, waiting for transfers between devices, sum_rows(): lax.psum_scatter(term(jnp.int32(0), count * lax.axis_size('tensor')).asty...  51.4 us
    unnamed x228, local copies, waits for them, and re-layouts  44.8 us
    all_gather x4, waiting for transfers between devices, gather_grad(): return lax.all_gather(rows_low, 'tensor', axis=0, tiled=True)  41.1 us
    reduce_scatter x4, waiting for transfers between devices, sum_back(): lax.psum_scatter(term(jnp.int32(0), count * lax.axis_size('tensor')).asty...  38.4 us
    dot_general x2, matrix products, block_forward(): pre = jnp.dot(full_first, in_w, preferred_element_type=jnp.float32)  25.4 us
    dot_general x6, matrix products, contract_rows(): lax.dot_general(left, right, (((0,), (0,)), ((), ())), preferred_element_...  23.6 us
  transfers between devices with their start and end apart: 14, of which 13 were waited for; matrix products, arithmetic and copies ran while one was open for 5% of the time, Pallas kernels for 0%

profile of v1, /device:TPU:1, one launch (start us, length us, event | category | flops | bytes accessed | tf_op | source)
XLA Modules:
  0.0 728.8 jit_solution(6761575692141350556)
XLA Ops:
  9.7 5.9 all-to-all-start
  17.6 3.5 convolution_convert_fusion.1
  42.9 14.0 %reduce-scatter.9.cloned.1.call-done = bf16[384,768]{1,0:T(8,128)(2,1)} async-done(((bf16[768,768]{1,0:T(8,128)(2,1)}), bf16[384,768]{1,0:T(8,128)(2,1)}) %reduce-scatter.9.cloned.1.call-update) | async-done | bytes 589840 | tf_op jit(solution)/shard_map/reduce_scatter | solution.py:74
  60.2 4.9 all_to_all.24
  65.1 12.7 %fusion.2 = (bf16[768,1536]{1,0:T(8,128)(2,1)S(1)}, f32[768,1536]{1,0:T(8,128)}) fusion(bf16[768,768]{1,0:T(8,128)(2,1)S(1)} %bitcast.140, bf16[768,1536]{1,0:T(8,128)(2,1)S(1)} %copy-done.83), kind=kOutput, calls=%fused_computation.6 | convolution fusion | flops 1888616448 | bytes 10616832 | tf_op jit(solution)/shard_map/dot_general | solution.py:156
  82.8 12.5 %reduce-scatter.11.cloned.1.call-done = bf16[384,768]{1,0:T(8,128)(2,1)} async-done(((bf16[768,768]{1,0:T(8,128)(2,1)}), bf16[384,768]{1,0:T(8,128)(2,1)}) %reduce-scatter.11.cloned.1.call-update) | async-done | bytes 589840 | tf_op jit(solution)/shard_map/reduce_scatter | solution.py:74
  99.5 5.1 all_to_all.25
  134.3 11.7 %reduce-scatter.13.cloned.1.call-done = bf16[384,768]{1,0:T(8,128)(2,1)} async-done(((bf16[768,768]{1,0:T(8,128)(2,1)}), bf16[384,768]{1,0:T(8,128)(2,1)}) %reduce-scatter.13.cloned.1.call-update) | async-done | bytes 589840 | tf_op jit(solution)/shard_map/reduce_scatter | solution.py:74
  150.2 4.6 all_to_all.26
  154.8 12.7 %fusion.5 = (bf16[768,1536]{1,0:T(8,128)(2,1)S(1)}, f32[768,1536]{1,0:T(8,128)}) fusion(bf16[768,768]{1,0:T(8,128)(2,1)S(1)} %bitcast.142, bf16[768,1536]{1,0:T(8,128)(2,1)S(1)} %copy-done), kind=kOutput, calls=%fused_computation.9 | convolution fusion | flops 1888616448 | bytes 10616832 | tf_op jit(solution)/shard_map/dot_general | solution.py:156
  172.0 13.1 %reduce-scatter.15.cloned.1.call-done = bf16[384,768]{1,0:T(8,128)(2,1)} async-done(((bf16[768,768]{1,0:T(8,128)(2,1)}), bf16[384,768]{1,0:T(8,128)(2,1)}) %reduce-scatter.15.cloned.1.call-update) | async-done | bytes 589840 | tf_op jit(solution)/shard_map/reduce_scatter | solution.py:74
  191.5 13.4 %all-gather.5.cloned.1.call-done = bf16[768,768]{1,0:T(8,128)(2,1)} async-done(((bf16[384,768]{1,0:T(8,128)(2,1)}), bf16[768,768]{1,0:T(8,128)(2,1)}) %all-gather.5.cloned.1.call-update) | async-done | bytes 1179664 | tf_op jit(solution)/shard_map/all_gather | solution.py:66
  204.8 5.4 fusion.11
  214.7 12.8 %reduce-scatter.17.cloned.1.call-done = bf16[384,768]{1,0:T(8,128)(2,1)} async-done(((bf16[768,768]{1,0:T(8,128)(2,1)}), bf16[384,768]{1,0:T(8,128)(2,1)}) %reduce-scatter.17.cloned.1.call-update) | async-done | bytes 589840 | tf_op jit(solution)/shard_map/reduce_scatter | solution.py:83
  233.7 12.4 %all-gather.7.cloned.1.call-done = bf16[768,768]{1,0:T(8,128)(2,1)} async-done(((bf16[384,768]{1,0:T(8,128)(2,1)}), bf16[768,768]{1,0:T(8,128)(2,1)}) %all-gather.7.cloned.1.call-update) | async-done | bytes 1179664 | tf_op jit(solution)/shard_map/all_gather | solution.py:66
  250.0 4.2 fusion.65
  278.1 12.8 %reduce-scatter.19.cloned.1.call-done = bf16[384,768]{1,0:T(8,128)(2,1)} async-done(((bf16[768,768]{1,0:T(8,128)(2,1)}), bf16[384,768]{1,0:T(8,128)(2,1)}) %reduce-scatter.19.cloned.1.call-update) | async-done | bytes 589840 | tf_op jit(solution)/shard_map/reduce_scatter | solution.py:83
  290.9 3.5 multiply_reduce_fusion.4
  295.9 13.1 %all-gather.9.cloned.1.call-done = bf16[768,768]{1,0:T(8,128)(2,1)} async-done(((bf16[384,768]{1,0:T(8,128)(2,1)}), bf16[768,768]{1,0:T(8,128)(2,1)}) %all-gather.9.cloned.1.call-update) | async-done | bytes 1179664 | tf_op jit(solution)/shard_map/all_gather | solution.py:66
  309.1 5.5 fusion.17
  319.1 12.8 %reduce-scatter.21.cloned.1.call-done = bf16[384,768]{1,0:T(8,128)(2,1)} async-done(((bf16[768,768]{1,0:T(8,128)(2,1)}), bf16[384,768]{1,0:T(8,128)(2,1)}) %reduce-scatter.21.cloned.1.call-update) | async-done | bytes 589840 | tf_op jit(solution)/shard_map/reduce_scatter | solution.py:83
  337.0 6.0 fusion.107
  343.0 4.3 fusion.108
  353.9 4.2 fusion.62
  383.4 4.2 fusion.104
  387.6 4.3 fusion.105
  393.6 4.7 convolution_bitcast_fusion.1
  399.1 70.0 %all-reduce = (f32[768]{0:T(1024)}, f32[768]{0:T(1024)}, f32[768]{0:T(1024)}, f32[768]{0:T(1024)}, f32[768]{0:T(1024)}, /*index=5*/f32[768]{0:T(1024)}, f32[768]{0:T(1024)}, f32[768]{0:T(1024)}) all-reduce(f32[768]{0:T(1024)S(1)} %get-tuple-element.82, f32[768]{0:T(1024)S(1)} %copy-done.72, ...), channel_id=1, replica_groups=mesh['dp'=64,'tensor'=2] {'dp','tensor'}, use_global_device_ids=true, to_apply=%region_34.35 | all-reduce | flops 6144 | bytes 49152 | tf_op jit(solution)/shard_map/psum | solution.py:282
  471.3 223.7 %all-reduce.4.cloned.1.call-done = (f32[3,768,384]{1,2,0:T(8,128)}, f32[384,768]{1,0:T(8,128)}, f32[768,1536]{1,0:T(8,128)}, f32[1536,768]{1,0:T(8,128)}, f32[3,...) async-done(((f32[3,768,384]{1,2,0:T(8,128)}, f32[384,768]{1,0:T(8,128)}, f32[768,1536]{1,0:T(8,128)}, f32[1536,768]{1,0:T(8,128)}, ...) | async-done | bytes 28311568 | tf_op jit(solution)/shard_map/psum | solution.py:267
  695.0 5.2 copy.167
  700.1 5.3 copy.168
  706.4 5.5 copy.222
  (368 shorter events, 179.7 us)
Async XLA Ops:
  7.2 147.6 %copy-start = (bf16[768,1536]{1,0:T(8,128)(2,1)S(1)}, bf16[768,1536]{1,0:T(8,128)(2,1)}, u32[]{:S(2)}) copy-start(bf16[768,1536]{1,0:T(8,128)(2,1)} %param.38) | copy-start | bytes 7077892
  9.7 7.9 %all-to-all-start = ((bf16[2,384,768]{2,1,0:T(8,128)(2,1)}), bf16[2,384,768]{2,1,0:T(8,128)(2,1)}, u32[]{:S(2)}, u32[]{:S(2)}) async-start(bf16[2,384,768]{2,1,0:T(8,128)(2,1)} %pad_maximum_fusion), calls=%async_computation | async-start | bytes 2359296 | tf_op jit(solution)/shard_map/all_to_all | solution.py:18
  15.6 41.3 %reduce-scatter.9.cloned.1.call-start = ((), (), s32[]{:S(2)}) async-start(), calls=%async_computation.12 | async-start | bytes 1769472 | tf_op jit(solution)/shard_map/reduce_scatter | solution.py:74
  25.7 9.5 %copy-start.10 = (bf16[3,256,6,64]{1,3,2,0:T(8,128)(2,1)}, bf16[3,256,6,64]{1,3,2,0:T(8,128)(2,1)S(1)}, u32[]{:S(2)}) copy-start(bf16[3,256,6,64]{1,3,2,0:T(8,128)(2,1)S(1)} %copy.123) | copy-start | bytes 1769476
  41.0 15.9 %copy-start.4 = (bf16[384,768]{1,0:T(8,128)(2,1)S(1)}, bf16[384,768]{1,0:T(8,128)(2,1)}, u32[]{:S(2)}) copy-start(bf16[384,768]{1,0:T(8,128)(2,1)} %param.21) | copy-start | bytes 1769476
  42.8 16.9 %copy-start.54 = (f32[768]{0:T(1024)S(1)}, f32[768]{0:T(1024)}, u32[]{:S(2)}) copy-start(f32[768]{0:T(1024)} %param.28) | copy-start | bytes 9220
  42.8 16.9 %copy-start.57 = (f32[768]{0:T(1024)S(1)}, f32[768]{0:T(1024)}, u32[]{:S(2)}) copy-start(f32[768]{0:T(1024)} %param.29) | copy-start | bytes 9220
  42.9 52.5 %reduce-scatter.11.cloned.1.call-start = ((), (), s32[]{:S(2)}) async-start(), calls=%async_computation.13 | async-start | bytes 1769472 | tf_op jit(solution)/shard_map/reduce_scatter | solution.py:74
  65.1 12.7 %copy-start.17 = (bf16[2,384,768]{2,1,0:T(8,128)(2,1)}, bf16[2,384,768]{2,1,0:T(8,128)(2,1)S(1)}, u32[]{:S(2)}) copy-start(bf16[2,384,768]{2,1,0:T(8,128)(2,1)S(1)} %all_to_all.24) | copy-start | bytes 3538948
  65.1 14.1 %copy-start.82 = (bf16[1536,768]{1,0:T(8,128)(2,1)S(1)}, bf16[1536,768]{1,0:T(8,128)(2,1)}, u32[]{:S(2)}) copy-start(bf16[1536,768]{1,0:T(8,128)(2,1)} %param.31) | copy-start | bytes 7077892
  82.2 63.8 %reduce-scatter.13.cloned.1.call-start = ((), (), s32[]{:S(2)}) async-start(), calls=%async_computation.14 | async-start | bytes 1769472 | tf_op jit(solution)/shard_map/reduce_scatter | solution.py:74
  131.0 15.0 %copy-start.60 = (f32[768]{0:T(1024)S(1)}, f32[768]{0:T(1024)}, u32[]{:S(2)}) copy-start(f32[768]{0:T(1024)} %param.32) | copy-start | bytes 9220
  132.9 52.2 %reduce-scatter.15.cloned.1.call-start = ((), (), s32[]{:S(2)}) async-start(), calls=%async_computation.15 | async-start | bytes 1769472 | tf_op jit(solution)/shard_map/reduce_scatter | solution.py:74
  154.8 12.7 %copy-start.19 = (bf16[2,384,768]{2,1,0:T(8,128)(2,1)}, bf16[2,384,768]{2,1,0:T(8,128)(2,1)S(1)}, u32[]{:S(2)}) copy-start(bf16[2,384,768]{2,1,0:T(8,128)(2,1)S(1)} %all_to_all.26) | copy-start | bytes 3538948
  154.8 14.1 %copy-start.81 = (bf16[1536,768]{1,0:T(8,128)(2,1)S(1)}, bf16[1536,768]{1,0:T(8,128)(2,1)}, u32[]{:S(2)}) copy-start(bf16[1536,768]{1,0:T(8,128)(2,1)} %param.39) | copy-start | bytes 7077892
  171.9 32.9 %all-gather.5.cloned.1.call-start = ((), (), s32[]{:S(2)}) async-start(), calls=%async_computation.16 | async-start | bytes 1769472 | tf_op jit(solution)/shard_map/all_gather | solution.py:66
  191.4 36.1 %reduce-scatter.17.cloned.1.call-start = ((), (), s32[]{:S(2)}) async-start(), calls=%async_computation.17 | async-start | bytes 1769472 | tf_op jit(solution)/shard_map/reduce_scatter | solution.py:83
  214.6 12.9 %copy-start.6 = (f32[384,768]{1,0:T(8,128)S(1)}, f32[384,768]{1,0:T(8,128)}, u32[]{:S(2)}) copy-start(f32[384,768]{1,0:T(8,128)} %copy-done.5) | copy-start | bytes 3538948
  214.7 15.6 %copy-start.9 = (f32[384,768]{1,0:T(8,128)S(1)}, f32[384,768]{1,0:T(8,128)}, u32[]{:S(2)}) copy-start(f32[384,768]{1,0:T(8,128)} %get-tuple-element.120) | copy-start | bytes 3538948
  214.7 31.4 %all-gather.7.cloned.1.call-start = ((), (), s32[]{:S(2)}) async-start(), calls=%async_computation.18 | async-start | bytes 1769472 | tf_op jit(solution)/shard_map/all_gather | solution.py:66
  232.6 58.3 %reduce-scatter.19.cloned.1.call-start = ((), (), s32[]{:S(2)}) async-start(), calls=%async_computation.19 | async-start | bytes 1769472 | tf_op jit(solution)/shard_map/reduce_scatter | solution.py:83
  233.6 20.5 %copy-start.47 = (f32[3,6,256]{2,1,0:T(8,128)}, f32[3,6,256]{2,1,0:T(8,128)S(1)}, u32[]{:S(2)}) copy-start(f32[3,6,256]{2,1,0:T(8,128)S(1)} %log_add_fusion.1) | copy-start | bytes 55300
  275.3 15.6 %copy-start.22 = (f32[384,768]{1,0:T(8,128)S(1)}, f32[384,768]{1,0:T(8,128)}, u32[]{:S(2)}) copy-start(f32[384,768]{1,0:T(8,128)} %get-tuple-element.118) | copy-start | bytes 3538948
  275.3 15.6 %copy-start.61 = (f32[768]{0:T(1024)S(1)}, f32[768]{0:T(1024)}, u32[]{:S(2)}) copy-start(f32[768]{0:T(1024)} %param.32) | copy-start | bytes 9220
  278.0 12.9 %copy-start.8 = (f32[384,768]{1,0:T(8,128)S(1)}, f32[384,768]{1,0:T(8,128)}, u32[]{:S(2)}) copy-start(f32[384,768]{1,0:T(8,128)} %get-tuple-element.126) | copy-start | bytes 3538948
  278.1 31.0 %all-gather.9.cloned.1.call-start = ((), (), s32[]{:S(2)}) async-start(), calls=%async_computation.20 | async-start | bytes 1769472 | tf_op jit(solution)/shard_map/all_gather | solution.py:66
  295.6 36.3 %reduce-scatter.21.cloned.1.call-start = ((), (), s32[]{:S(2)}) async-start(), calls=%async_computation.21 | async-start | bytes 1769472 | tf_op jit(solution)/shard_map/reduce_scatter | solution.py:83
  319.1 30.5 %all-gather.11.cloned.1.call-start = ((), (), s32[]{:S(2)}) async-start(), calls=%async_computation.22 | async-start | bytes 1769472 | tf_op jit(solution)/shard_map/all_gather | solution.py:66
  336.1 132.9 %reduce-scatter.23.cloned.1.call-start = ((), (), s32[]{:S(2)}) async-start(), calls=%async_computation.23 | async-start | bytes 1769472 | tf_op jit(solution)/shard_map/reduce_scatter | solution.py:83
  376.6 318.4 %all-reduce.4.cloned.1.call-start = ((), (), s32[]{:S(2)}) async-start(), calls=%async_computation.24 | async-start | bytes 56623104 | tf_op jit(solution)/shard_map/psum | solution.py:267
  398.3 70.7 %copy-start.21 = (f32[384,768]{1,0:T(8,128)S(1)}, f32[384,768]{1,0:T(8,128)}, u32[]{:S(2)}) copy-start(f32[384,768]{1,0:T(8,128)} %get-tuple-element.113) | copy-start | bytes 3538948
  700.1 11.8 %slice-start.8 = ((s8[4718592]{0:T(1024)(128)(4,1)}), s8[524288]{0:T(1024)(128)(4,1)S(1)}, s32[]{:S(2)}) async-start(s8[4718592]{0:T(1024)(128)(4,1)} %bitcast.138), calls=%async_computation.33 | async-start | bytes 1048576
  (89 other events, 263.3 us)
Sparse Core Ops, SparseCore 0:
  43.0 13.9 reduce-scatter.8
  82.4 12.9 reduce-scatter.10
  133.0 12.9 reduce-scatter.12
  172.0 12.9 reduce-scatter.14
  191.5 13.2 all-gather.4
  214.8 12.6 reduce-scatter.16
  232.7 13.2 all-gather.6
  278.2 12.6 reduce-scatter.18
  295.8 13.2 all-gather.8
  319.2 12.6 reduce-scatter.20
  336.2 13.2 all-gather.10
  376.7 12.6 reduce-scatter.22
  398.5 296.4 all-reduce.3
